TPU v7x, 32 devices: a whole 2x2x4 slice. The times are simulated.
32 devices in a mesh: groups: 2 (over x), row: 16 (over z, y, core).
Axes of the slice: x: 2, y: 2, z: 4, core: 2. Of those that a mesh axis runs over, the one named last changes fastest.
Arguments:
- pair_rows: bfloat16 [256, 128, 128], P(('groups', 'row')), parts along dimension 0, may hold values from -6 to 6
- in_gain: float32 [128], replicated, may hold values from 0.1 to 1.9
- w_left: bfloat16 [128, 128], replicated, may hold values from -0.5 to 0.5
- w_left_gate: bfloat16 [128, 128], replicated, may hold values from -0.5 to 0.5
- w_right: bfloat16 [128, 128], replicated, may hold values from -0.5 to 0.5
- w_right_gate: bfloat16 [128, 128], replicated, may hold values from -0.5 to 0.5
- w_gate: bfloat16 [128, 128], replicated, may hold values from -0.5 to 0.5
- w_out: bfloat16 [128, 128], replicated, may hold values from -0.5 to 0.5
- out_gain: float32 [128], replicated, may hold values from 0.1 to 1.9
- valid_len: int32 [2], P('groups'), parts along dimension 0, may hold values from 64 to 128
- window: int32 [2], P('groups'), parts along dimension 0, may hold values from 0 to 7
Outputs:
- update: bfloat16 [256, 16, 128], P(('groups', 'row')), parts along dimension 0
There are 2 independent parts, one for each index of `groups`. A program takes and returns all parts, laid end to end along the dimension named above; an argument that names none is the same for every part. Nothing has to cross between parts.
All inputs are finite; a program needn't handle non-finite values.
Results may differ from a plain program's by a relative error of at most 0.0078.
Values may be sent and summed in bfloat16 or wider, within the bound.
A program may use at most 128 MiB of HBM per device.

v0:
```python
import jax
import jax.numpy as jnp
from jax import lax
from jax.sharding import PartitionSpec as P


def layer_norm(values, gain):
    mean_v = jnp.mean(values, axis=-1, keepdims=True)
    centered = values - mean_v
    variance_v = jnp.mean(centered * centered, axis=-1, keepdims=True)
    return centered * lax.rsqrt(variance_v + 1e-05) * gain


def on_device(
    pair_rows,
    in_gain,
    w_left,
    w_left_gate,
    w_right,
    w_right_gate,
    w_gate,
    w_out,
    out_gain,
    valid_len,
    window,
):
    my_index = lax.axis_index("row")
    local_rows, tokens_all, channels = pair_rows.shape
    width_win = tokens_all // 8
    valid_upto = valid_len[0]
    start_block = window[0]
    start_row = start_block * width_win
    row_ids = my_index * local_rows + jnp.arange(local_rows, dtype=jnp.int32)
    row_live = (row_ids < valid_upto).astype(jnp.float32)
    col_live = (jnp.arange(tokens_all, dtype=jnp.int32) < valid_upto).astype(jnp.float32)
    live_mask = (row_live[:, None] * col_live[None, :])[:, :, None]
    normed = layer_norm(pair_rows.astype(jnp.float32), in_gain).astype(jnp.bfloat16)
    flat_rows = normed.reshape(-1, channels)
    joined = jnp.concatenate([w_left, w_left_gate, w_right, w_right_gate], axis=1)
    projected = jnp.dot(flat_rows, joined, preferred_element_type=jnp.float32)
    projected = projected.reshape(local_rows, tokens_all, 4 * channels)
    left_edge = (
        jax.nn.sigmoid(projected[:, :, channels : 2 * channels])
        * projected[:, :, :channels]
        * live_mask
    ).astype(jnp.bfloat16)
    right_edge = (
        jax.nn.sigmoid(projected[:, :, 3 * channels :])
        * projected[:, :, 2 * channels : 3 * channels]
        * live_mask
    ).astype(jnp.bfloat16)
    gate_in = lax.dynamic_slice_in_dim(normed, start_row, width_win, 1)
    gate_vals = jax.nn.sigmoid(
        jnp.dot(gate_in.reshape(-1, channels), w_gate, preferred_element_type=jnp.float32)
    )
    gate_vals = gate_vals.reshape(local_rows, width_win, channels)
    regrouped = lax.all_to_all(right_edge, "row", split_axis=1, concat_axis=0, tiled=True)
    picked = lax.dynamic_slice_in_dim(regrouped, start_row, width_win, 0)
    window_right = lax.all_gather(picked, "row", axis=1, tiled=True)
    product = jnp.einsum(
        "ikc,jkc->ijc", left_edge, window_right, preferred_element_type=jnp.float32
    )
    normed_out = layer_norm(product, out_gain).astype(jnp.bfloat16)
    result = jnp.dot(normed_out.reshape(-1, channels), w_out, preferred_element_type=jnp.float32)
    return (gate_vals * result.reshape(local_rows, width_win, channels)).astype(jnp.bfloat16)


def solution(mesh):
    return jax.shard_map(
        on_device,
        mesh=mesh,
        in_specs=(
            P(("groups", "row"), None, None),
            P(),
            P(),
            P(),
            P(),
            P(),
            P(),
            P(),
            P(),
            P("groups"),
            P("groups"),
        ),
        out_specs=P(("groups", "row"), None, None),
        check_vma=False,
    )
```

profile of v0, /device:TPU:9, one launch (start us, length us, event | category | flops | bytes accessed | tf_op | source)
XLA Modules:
  0.0 75.5 jit_solution(6741622553419118071)
XLA Ops:
  0.0 0.0 copy-start
  0.7 1.1 %convert_reduce_fusion = f32[8,128]{1,0:T(8,128)S(1)} fusion(bf16[8,128,128]{2,1,0:T(8,128)(2,1)} %param.11), kind=kLoop, calls=%fused_computation.7 | loop fusion | flops 261120 | bytes 266240 | tf_op jit(solution)/shard_map/reduce_sum | solution.py:8
  1.8 1.3 %fusion.6 = f32[8,128]{1,0:T(8,128)S(1)} fusion(bf16[8,128,128]{2,1,0:T(8,128)(2,1)} %param.11, f32[8,128]{1,0:T(8,128)S(1)} %broadcast_multiply_fusion.2), kind=kLoop, calls=%fused_computation.10 | loop fusion | flops 523264 | bytes 270336 | tf_op jit(solution)/shard_map/reduce_sum | solution.py:10
  3.1 0.1 broadcast_multiply_fusion.1
  3.2 1.3 %fusion.8 = bf16[8,128,128]{2,1,0:T(8,128)(2,1)S(1)} fusion(bf16[8,128,128]{2,1,0:T(8,128)(2,1)} %param.11, f32[128]{0:T(128)} %param.12, f32[8,128]{1,0:T(8,128)S(1)} %add_rsqrt_fusion.1, f32[8,128]{1,0:T(8,128)S(1)} %broadcast_multiply_fusion.2), kind=kLoop, calls=%fused_computation.12 | loop fusion | flops 655360 | bytes 532992 | tf_op jit(solution)/shard_map/convert_element_type | solution.py:37
  4.5 1.2 %fusion.19 = f32[8,128,512]{2,1,0:T(8,128)S(1)} fusion(bf16[8,128,128]{2,1,0:T(8,128)(2,1)S(1)} %fusion.8, bf16[128,128]{1,0:T(8,128)(2,1)} %param.16, bf16[128,128]{1,0:T(8,128)(2,1)} %param.15, bf16[128,128]{1,0:T(8,128)(2,1)} %param.14, bf16[128,128]{1,0:T(8,128)(2,1)} %param.13), kind=kOutput, calls=%fused_computation.28 | convolution fusion | flops 134742016 | bytes 2490368 | tf_op jit(solution)/shard_map/dot_general | solution.py:40
  5.7 0.3 fusion.10
  6.0 0.9 %copy.29 = bf16[8,128,128]{2,0,1:T(8,128)(2,1)} copy(bf16[8,128,128]{2,1,0:T(8,128)(2,1)S(1)} %get-tuple-element.6) | data formatting | bytes 524288 | tf_op jit(solution)/shard_map/convert_element_type | solution.py:51
  6.9 6.6 %all-to-all-start = ((bf16[8,128,128]{2,0,1:T(8,128)(2,1)}), bf16[8,128,128]{2,0,1:T(8,128)(2,1)S(1)}, u32[]{:S(2)}, u32[]{:S(2)}) async-start(bf16[8,128,128]{2,0,1:T(8,128)(2,1)} %copy.29), calls=%async_computation | async-start | bytes 524288 | tf_op jit(solution)/shard_map/all_to_all | solution.py:57
  14.1 0.2 copy.33
  14.4 0.0 copy-done
  14.4 0.2 fusion.2
  14.5 7.6 %all-to-all-done = bf16[8,128,128]{2,0,1:T(8,128)(2,1)S(1)} async-done(((bf16[8,128,128]{2,0,1:T(8,128)(2,1)}), bf16[8,128,128]{2,0,1:T(8,128)(2,1)S(1)}, u32[]{:S(2)}, u32[]{:S(2)}) %all-to-all-start) | async-done | bytes 262176 | tf_op jit(solution)/shard_map/all_to_all | solution.py:57
  22.2 0.2 copy.36
  22.4 0.0 copy-start.1
  22.5 0.0 copy-start.2
  22.5 50.5 %all_gather.3 = bf16[16,128,128]{0,1,2:T(8,128)(2,1)S(1)} all-gather(bf16[16,8,128]{0,1,2:T(8,128)(2,1)S(1)} %copy.36), channel_id=1, replica_groups=mesh['groups'=2,'row'=16] {'row'}, dimensions={1}, use_global_device_ids=true | all-gather | bytes 557056 | tf_op jit(solution)/shard_map/all_gather | solution.py:59
  73.0 1.2 %fusion.31 = f32[128,16,8]{1,2,0:T(8,128)S(1)} fusion(bf16[16,128,128]{0,1,2:T(8,128)(2,1)S(1)} %all_gather.3, bf16[8,128,128]{1,0,2:T(8,128)(2,1)S(1)} %copy.33), kind=kOutput, calls=%fused_computation.53 | convolution fusion | flops 4194304 | bytes 851968 | tf_op jit(solution)/shard_map/ikc,jkc->ijc/dot_general | solution.py:60
  74.2 0.2 copy.34
  74.4 0.1 bitcast_reduce_fusion
  74.5 0.2 multiply_reduce_fusion
  74.7 0.0 copy-done.1
  74.7 0.0 copy-done.2
  74.7 0.8 %fusion.3 = bf16[8,16,128]{2,1,0:T(8,128)(2,1)} fusion(f32[8,16,128]{2,1,0:T(8,128)S(1)} %bitcast.31, f32[128,16,8]{0,1,2:T(8,128)S(1)} %copy.34, bf16[128,128]{1,0:T(8,128)(2,1)S(1)} %copy-done.1, f32[128]{0:T(128)S(1)} %copy-done.2, f32[8,16]{1,0:T(8,128)S(1)} %add_rsqrt_fusion, f32[8,16]{1,0:T(8,128)S(1)} %broadcast_multiply_fusion), kind=kOutput, calls=%fused_computation.5 | convolution fusion | flops 4292608 | bytes 198144 | tf_op jit(solution)/shard_map/dot_general | solution.py:64
  (9 shorter events, 0.1 us)
Async XLA Ops:
  0.0 14.4 %copy-start = (bf16[128,128]{1,0:T(8,128)(2,1)S(1)}, bf16[128,128]{1,0:T(8,128)(2,1)}, u32[]{:S(2)}) copy-start(bf16[128,128]{1,0:T(8,128)(2,1)} %param.17) | copy-start | bytes 98308
  6.9 15.3 %all-to-all-start = ((bf16[8,128,128]{2,0,1:T(8,128)(2,1)}), bf16[8,128,128]{2,0,1:T(8,128)(2,1)S(1)}, u32[]{:S(2)}, u32[]{:S(2)}) async-start(bf16[8,128,128]{2,0,1:T(8,128)(2,1)} %copy.29), calls=%async_computation | async-start | bytes 524288 | tf_op jit(solution)/shard_map/all_to_all | solution.py:57
  22.4 52.2 %copy-start.1 = (bf16[128,128]{1,0:T(8,128)(2,1)S(1)}, bf16[128,128]{1,0:T(8,128)(2,1)}, u32[]{:S(2)}) copy-start(bf16[128,128]{1,0:T(8,128)(2,1)} %param.18) | copy-start | bytes 98308
  22.5 52.2 %copy-start.2 = (f32[128]{0:T(128)S(1)}, f32[128]{0:T(128)}, u32[]{:S(2)}) copy-start(f32[128]{0:T(128)} %param.19) | copy-start | bytes 1540
where the time goes:
time: 76 us; the launch traced here: 75.5 us
  blocking collectives  50.5 us (66%)
  waiting for transfers between devices  7.63 us (10%)
  starting transfers between devices  6.58 us (9%)
  other arithmetic  4.38 us (6%)
  matrix products  3.4 us (4%)
  local copies, waits for them, and re-layouts  1.53 us (2%)
  between operations  1.5 us (2%)
    all_gather x1, blocking collectives, on_device(): window_right = lax.all_gather(picked, 'row', axis=1, tiled=True)  50.5 us
    all_to_all x1, waiting for transfers between devices, on_device(): lax.all_to_all(right_edge, 'row', split_axis=1, concat_axis=0, tiled=True)  7.63 us
    all_to_all x1, starting transfers between devices, on_device(): lax.all_to_all(right_edge, 'row', split_axis=1, concat_axis=0, tiled=True)  6.58 us
  transfers between devices with their start and end apart: 1, of which 1 were waited for; matrix products, arithmetic and copies ran while one was open for 0% of the time, Pallas kernels for 0%

commit v1 on v0

--- a/solution.py
+++ b/solution.py
@@ -56,7 +56,16 @@
     gate_vals = gate_vals.reshape(local_rows, width_win, channels)
     regrouped = lax.all_to_all(right_edge, "row", split_axis=1, concat_axis=0, tiled=True)
     picked = lax.dynamic_slice_in_dim(regrouped, start_row, width_win, 0)
-    window_right = lax.all_gather(picked, "row", axis=1, tiled=True)
+    ways = lax.axis_size("row")
+    up = [(d, (d + 1) % ways) for d in range(ways)]
+    down = [(d, (d - 1) % ways) for d in range(ways)]
+    earlier, later = ([picked], [picked])
+    for _ in range(ways // 2):
+        earlier.append(lax.ppermute(earlier[-1], "row", up))
+    for _ in range((ways - 1) // 2):
+        later.append(lax.ppermute(later[-1], "row", down))
+    line = jnp.concatenate([*earlier[::-1], *later[1:]], axis=1)
+    window_right = jnp.roll(line, (lax.axis_index("row") - ways // 2) * picked.shape[1], axis=1)
     product = jnp.einsum(
         "ikc,jkc->ijc", left_edge, window_right, preferred_element_type=jnp.float32
     )

time: 76 us -> 156 us (2.05); the launches traced: 75.5 us -> 154 us
  waiting for transfers between devices: 7.63 us -> 93.5 us
  blocking collectives: 50.5 us -> 0 us
  local copies, waits for them, and re-layouts: 1.53 us -> 26.6 us
  starting transfers between devices: 6.58 us -> 24.2 us
    ppermute x0 -> x15, waiting for transfers between devices: none -> 85.5 us  [the longest x7 63.9 us: on_device(): later.append(lax.ppermute(later[-1], 'row', down))]
    all_gather x1 -> x0, blocking collectives: 50.5 us -> none  [on_device(): window_right = lax.all_gather(picked, 'row', axis=1, tiled=True)]
    ppermute x0 -> x15, starting transfers between devices: none -> 17.6 us  [the longest x8 17.6 us: on_device(): earlier.append(lax.ppermute(earlier[-1], 'row', up))]
    concatenate x0 -> x1, local copies, waits for them, and re-layouts: none -> 15.7 us  [on_device(): jnp.roll(line, (lax.axis_index('row') - ways // 2) * picked.shape[1], axi...]
    all_to_all x1, local copies, waits for them, and re-layouts: 0.04 us -> 7.22 us  [on_device(): lax.all_to_all(right_edge, 'row', split_axis=1, concat_axis=0, tiled=True)]
  transfers between devices with their start and end apart: 1 -> 16, of which waited for: 1 -> 16; matrix products, arithmetic and copies ran while one was open for 0% -> 1% of each run, Pallas kernels for 0% -> 0%
where the time goes in v1:
time: 156 us; the launch traced here: 154 us
  waiting for transfers between devices  93.5 us (60%)
  local copies, waits for them, and re-layouts  26.6 us (17%)
  starting transfers between devices  24.2 us (16%)
  other arithmetic  5.09 us (3%)
  matrix products  2.67 us (2%)
    ppermute x7, waiting for transfers between devices, on_device(): later.append(lax.ppermute(later[-1], 'row', down))  63.9 us
    ppermute x8, waiting for transfers between devices, on_device(): earlier.append(lax.ppermute(earlier[-1], 'row', up))  21.6 us
    ppermute x8, starting transfers between devices, on_device(): earlier.append(lax.ppermute(earlier[-1], 'row', up))  17.6 us
    concatenate x1, local copies, waits for them, and re-layouts, on_device(): jnp.roll(line, (lax.axis_index('row') - ways // 2) * picked.shape[1], axi...  15.7 us
    all_to_all x1, waiting for transfers between devices, on_device(): lax.all_to_all(right_edge, 'row', split_axis=1, concat_axis=0, tiled=True)  8.02 us
    all_to_all x1, local copies, waits for them, and re-layouts, on_device(): lax.all_to_all(right_edge, 'row', split_axis=1, concat_axis=0, tiled=True)  7.22 us
    all_to_all x1, starting transfers between devices, on_device(): lax.all_to_all(right_edge, 'row', split_axis=1, concat_axis=0, tiled=True)  6.58 us
  transfers between devices with their start and end apart: 16, of which 16 were waited for; matrix products, arithmetic and copies ran while one was open for 1% of the time, Pallas kernels for 0%

profile of v1, /device:TPU:9, one launch (start us, length us, event | category | flops | bytes accessed | tf_op | source)
XLA Modules:
  0.0 153.6 jit_solution(5014534823333903058)
XLA Ops:
  0.7 1.1 convert_reduce_fusion
  1.8 1.3 fusion.6
  3.1 0.1 broadcast_multiply_fusion.1
  3.2 1.3 fusion.8
  4.5 1.2 fusion.21
  5.7 1.0 fusion.15
  6.8 0.9 copy.19
  7.6 6.6 %all-to-all-start = ((bf16[8,128,128]{2,0,1:T(8,128)(2,1)}), bf16[8,128,128]{2,0,1:T(8,128)(2,1)S(1)}, u32[]{:S(2)}, u32[]{:S(2)}) async-start(bf16[8,128,128]{2,0,1:T(8,128)(2,1)} %copy.19), calls=%async_computation | async-start | bytes 524288 | tf_op jit(solution)/shard_map/all_to_all | solution.py:57
  14.9 8.0 %all-to-all-done = bf16[8,128,128]{2,0,1:T(8,128)(2,1)S(1)} async-done(((bf16[8,128,128]{2,0,1:T(8,128)(2,1)}), bf16[8,128,128]{2,0,1:T(8,128)(2,1)S(1)}, u32[]{:S(2)}, u32[]{:S(2)}) %all-to-all-start) | async-done | bytes 262176 | tf_op jit(solution)/shard_map/all_to_all | solution.py:57
  22.9 7.2 %copy.20 = bf16[8,16,8,128]{2,0,1,3:T(8,128)(2,1)} copy(bf16[8,16,8,128]{3,0,2,1:T(8,128)(2,1)S(1)} %bitcast.29) | data formatting | bytes 524288 | tf_op jit(solution)/shard_map/all_to_all | solution.py:57
  30.1 1.1 constant_dynamic-slice_fusion
  31.2 0.5 collective-permute-start
  31.7 0.1 collective-permute-start.8
  31.7 11.7 %collective-permute-done = bf16[16,8,128]{1,0,2:T(8,128)(2,1)S(1)} collective-permute-done((bf16[16,8,128]{1,0,2:T(8,128)(2,1)S(1)}, bf16[16,8,128]{1,0,2:T(8,128)(2,1)S(1)}, u32[]{:S(2)}, u32[]{:S(2)}) %collective-permute-start) | collective-permute-done | bytes 32800 | tf_op jit(solution)/shard_map/ppermute | solution.py:64
  43.4 2.5 %collective-permute-start.1 = (bf16[16,8,128]{1,0,2:T(8,128)(2,1)S(1)}, bf16[16,8,128]{1,0,2:T(8,128)(2,1)S(1)}, u32[]{:S(2)}, u32[]{:S(2)}) collective-permute-start(bf16[16,8,128]{1,0,2:T(8,128)(2,1)S(1)} %collective-permute-done), channel_id=1, source_target_pairs={{0,1},{1,2},{2,3},{3,4},{4,5},{5,6},{6,7},{7,8},{8,9},{9,10},{10,1... | collective-permute-start | bytes 98312 | tf_op jit(solution)/shard_map/ppermute | solution.py:64
  45.9 4.7 %collective-permute-done.8 = bf16[16,8,128]{1,0,2:T(8,128)(2,1)S(1)} collective-permute-done((bf16[16,8,128]{1,0,2:T(8,128)(2,1)S(1)}, bf16[16,8,128]{1,0,2:T(8,128)(2,1)S(1)}, u32[]{:S(2)}, u32[]{:S(2)}) %collective-permute-start.8) | collective-permute-done | bytes 32800 | tf_op jit(solution)/shard_map/ppermute | solution.py:66
  50.6 5.7 %collective-permute-done.1 = bf16[16,8,128]{1,0,2:T(8,128)(2,1)S(1)} collective-permute-done((bf16[16,8,128]{1,0,2:T(8,128)(2,1)S(1)}, bf16[16,8,128]{1,0,2:T(8,128)(2,1)S(1)}, u32[]{:S(2)}, u32[]{:S(2)}) %collective-permute-start.1) | collective-permute-done | bytes 32800 | tf_op jit(solution)/shard_map/ppermute | solution.py:64
  56.3 2.5 %collective-permute-start.2 = (bf16[16,8,128]{1,0,2:T(8,128)(2,1)S(1)}, bf16[16,8,128]{1,0,2:T(8,128)(2,1)S(1)}, u32[]{:S(2)}, u32[]{:S(2)}) collective-permute-start(bf16[16,8,128]{1,0,2:T(8,128)(2,1)S(1)} %collective-permute-done.1), channel_id=1, source_target_pairs={{0,1},{1,2},{2,3},{3,4},{4,5},{5,6},{6,7},{7,8},{8,9},{9,10},{10,1... | collective-permute-start | bytes 98312 | tf_op jit(solution)/shard_map/ppermute | solution.py:64
  58.8 11.0 %collective-permute-done.9 = bf16[16,8,128]{1,0,2:T(8,128)(2,1)S(1)} collective-permute-done((bf16[16,8,128]{1,0,2:T(8,128)(2,1)S(1)}, bf16[16,8,128]{1,0,2:T(8,128)(2,1)S(1)}, u32[]{:S(2)}, u32[]{:S(2)}) %collective-permute-start.9) | collective-permute-done | bytes 32800 | tf_op jit(solution)/shard_map/ppermute | solution.py:66
  69.8 0.7 collective-permute-done.2
  70.5 0.1 copy-done.1
  70.6 2.4 %collective-permute-start.3 = (bf16[16,8,128]{1,0,2:T(8,128)(2,1)S(1)}, bf16[16,8,128]{1,0,2:T(8,128)(2,1)S(1)}, u32[]{:S(2)}, u32[]{:S(2)}) collective-permute-start(bf16[16,8,128]{1,0,2:T(8,128)(2,1)S(1)} %collective-permute-done.2), channel_id=1, source_target_pairs={{0,1},{1,2},{2,3},{3,4},{4,5},{5,6},{6,7},{7,8},{8,9},{9,10},{10,1... | collective-permute-start | bytes 98312 | tf_op jit(solution)/shard_map/ppermute | solution.py:64
  73.0 11.0 %collective-permute-done.10 = bf16[16,8,128]{1,0,2:T(8,128)(2,1)S(1)} collective-permute-done((bf16[16,8,128]{1,0,2:T(8,128)(2,1)S(1)}, bf16[16,8,128]{1,0,2:T(8,128)(2,1)S(1)}, u32[]{:S(2)}, u32[]{:S(2)}) %collective-permute-start.10) | collective-permute-done | bytes 32800 | tf_op jit(solution)/shard_map/ppermute | solution.py:66
  84.0 0.7 collective-permute-done.3
  84.7 0.1 copy-done.3
  84.8 2.4 %collective-permute-start.4 = (bf16[16,8,128]{1,0,2:T(8,128)(2,1)S(1)}, bf16[16,8,128]{1,0,2:T(8,128)(2,1)S(1)}, u32[]{:S(2)}, u32[]{:S(2)}) collective-permute-start(bf16[16,8,128]{1,0,2:T(8,128)(2,1)S(1)} %collective-permute-done.3), channel_id=1, source_target_pairs={{0,1},{1,2},{2,3},{3,4},{4,5},{5,6},{6,7},{7,8},{8,9},{9,10},{10,1... | collective-permute-start | bytes 98312 | tf_op jit(solution)/shard_map/ppermute | solution.py:64
  87.2 11.0 %collective-permute-done.11 = bf16[16,8,128]{1,0,2:T(8,128)(2,1)S(1)} collective-permute-done((bf16[16,8,128]{1,0,2:T(8,128)(2,1)S(1)}, bf16[16,8,128]{1,0,2:T(8,128)(2,1)S(1)}, u32[]{:S(2)}, u32[]{:S(2)}) %collective-permute-start.11) | collective-permute-done | bytes 32800 | tf_op jit(solution)/shard_map/ppermute | solution.py:66
  98.3 0.7 collective-permute-done.4
  99.0 0.1 copy-done.5
  99.0 2.4 %collective-permute-start.5 = (bf16[16,8,128]{1,0,2:T(8,128)(2,1)S(1)}, bf16[16,8,128]{1,0,2:T(8,128)(2,1)S(1)}, u32[]{:S(2)}, u32[]{:S(2)}) collective-permute-start(bf16[16,8,128]{1,0,2:T(8,128)(2,1)S(1)} %collective-permute-done.4), channel_id=1, source_target_pairs={{0,1},{1,2},{2,3},{3,4},{4,5},{5,6},{6,7},{7,8},{8,9},{9,10},{10,1... | collective-permute-start | bytes 98312 | tf_op jit(solution)/shard_map/ppermute | solution.py:64
  101.5 11.0 %collective-permute-done.12 = bf16[16,8,128]{1,0,2:T(8,128)(2,1)S(1)} collective-permute-done((bf16[16,8,128]{1,0,2:T(8,128)(2,1)S(1)}, bf16[16,8,128]{1,0,2:T(8,128)(2,1)S(1)}, u32[]{:S(2)}, u32[]{:S(2)}) %collective-permute-start.12) | collective-permute-done | bytes 32800 | tf_op jit(solution)/shard_map/ppermute | solution.py:66
  112.5 0.7 collective-permute-done.5
  113.2 0.1 copy-done.7
  113.3 2.4 %collective-permute-start.6 = (bf16[16,8,128]{1,0,2:T(8,128)(2,1)S(1)}, bf16[16,8,128]{1,0,2:T(8,128)(2,1)S(1)}, u32[]{:S(2)}, u32[]{:S(2)}) collective-permute-start(bf16[16,8,128]{1,0,2:T(8,128)(2,1)S(1)} %collective-permute-done.5), channel_id=1, source_target_pairs={{0,1},{1,2},{2,3},{3,4},{4,5},{5,6},{6,7},{7,8},{8,9},{9,10},{10,1... | collective-permute-start | bytes 98312 | tf_op jit(solution)/shard_map/ppermute | solution.py:64
  115.7 11.0 %collective-permute-done.13 = bf16[16,8,128]{1,0,2:T(8,128)(2,1)S(1)} collective-permute-done((bf16[16,8,128]{1,0,2:T(8,128)(2,1)S(1)}, bf16[16,8,128]{1,0,2:T(8,128)(2,1)S(1)}, u32[]{:S(2)}, u32[]{:S(2)}) %collective-permute-start.13) | collective-permute-done | bytes 32800 | tf_op jit(solution)/shard_map/ppermute | solution.py:66
  126.7 0.7 collective-permute-done.6
  127.4 2.5 %collective-permute-start.7 = (bf16[16,8,128]{1,0,2:T(8,128)(2,1)S(1)}, bf16[16,8,128]{1,0,2:T(8,128)(2,1)}, u32[]{:S(2)}, u32[]{:S(2)}) collective-permute-start(bf16[16,8,128]{1,0,2:T(8,128)(2,1)S(1)} %collective-permute-done.6), channel_id=1, source_target_pairs={{0,1},{1,2},{2,3},{3,4},{4,5},{5,6},{6,7},{7,8},{8,9},{9,10},{10,1... | collective-permute-start | bytes 98312 | tf_op jit(solution)/shard_map/ppermute | solution.py:64
  129.9 0.2 fusion.2
  130.1 1.1 copy.21
  131.3 0.0 copy-start.12
  131.3 4.2 %collective-permute-done.14 = bf16[16,8,128]{1,0,2:T(8,128)(2,1)} collective-permute-done((bf16[16,8,128]{1,0,2:T(8,128)(2,1)S(1)}, bf16[16,8,128]{1,0,2:T(8,128)(2,1)}, u32[]{:S(2)}, u32[]{:S(2)}) %collective-permute-start.14) | collective-permute-done | bytes 32800 | tf_op jit(solution)/shard_map/ppermute | solution.py:66
  135.4 0.6 collective-permute-done.7
  136.0 15.7 %concatenate.10 = bf16[16,256,128]{1,0,2:T(8,128)(2,1)S(1)} concatenate(bf16[16,8,128]{1,0,2:T(8,128)(2,1)} %collective-permute-done.7, bf16[16,8,128]{1,0,2:T(8,128)(2,1)} %copy-done.10, bf16[16,8,128]{1,0,2:T(8,128)(2,1)} %copy-done.8, bf16[16,8,128]{1,0,2:T(8,128)(2,1)} %copy-done.6, bf16[16,8,128]{1,0,2:T(8,128)(2,1)} %copy-done.4, bf16[16,8,128]{1,0,2:T(8,128)(2,1)} %copy-done.2, ...), dimensions={1} | concatenate | bytes 2097152 | tf_op jit(solution)/shard_map/jit(_roll_dynamic)/concatenate | solution.py:68
  151.8 0.5 fusion.19
  152.3 0.2 copy.22
  152.4 0.1 bitcast_reduce_fusion
  152.6 0.2 multiply_reduce_fusion
  152.8 0.8 fusion.3
  (34 shorter events, 0.1 us)
Async XLA Ops:
  0.0 129.9 %copy-start = (bf16[128,128]{1,0:T(8,128)(2,1)S(1)}, bf16[128,128]{1,0:T(8,128)(2,1)}, u32[]{:S(2)}) copy-start(bf16[128,128]{1,0:T(8,128)(2,1)} %param.17) | copy-start | bytes 98308
  7.6 15.3 %all-to-all-start = ((bf16[8,128,128]{2,0,1:T(8,128)(2,1)}), bf16[8,128,128]{2,0,1:T(8,128)(2,1)S(1)}, u32[]{:S(2)}, u32[]{:S(2)}) async-start(bf16[8,128,128]{2,0,1:T(8,128)(2,1)} %copy.19), calls=%async_computation | async-start | bytes 524288 | tf_op jit(solution)/shard_map/all_to_all | solution.py:57
  31.2 12.3 %collective-permute-start = (bf16[16,8,128]{1,0,2:T(8,128)(2,1)S(1)}, bf16[16,8,128]{1,0,2:T(8,128)(2,1)S(1)}, u32[]{:S(2)}, u32[]{:S(2)}) collective-permute-start(bf16[16,8,128]{1,0,2:T(8,128)(2,1)S(1)} %constant_dynamic-slice_fusion), channel_id=1, source_target_pairs={{0,1},{1,2},{2,3},{3,4},{4,5},{5,6},{6,7},{7,8},{8,9},{9,10},{10,1... | collective-permute-start | bytes 98312 | tf_op jit(solution)/shard_map/ppermute | solution.py:64
  31.7 18.9 %collective-permute-start.8 = (bf16[16,8,128]{1,0,2:T(8,128)(2,1)S(1)}, bf16[16,8,128]{1,0,2:T(8,128)(2,1)S(1)}, u32[]{:S(2)}, u32[]{:S(2)}) collective-permute-start(bf16[16,8,128]{1,0,2:T(8,128)(2,1)S(1)} %constant_dynamic-slice_fusion), channel_id=1, source_target_pairs={{0,15},{1,0},{2,1},{3,2},{4,3},{5,4},{6,5},{7,6},{8,7},{9,8},{10,9... | collective-permute-start | bytes 98312 | tf_op jit(solution)/shard_map/ppermute | solution.py:66
  43.4 12.8 %collective-permute-start.1 = (bf16[16,8,128]{1,0,2:T(8,128)(2,1)S(1)}, bf16[16,8,128]{1,0,2:T(8,128)(2,1)S(1)}, u32[]{:S(2)}, u32[]{:S(2)}) collective-permute-start(bf16[16,8,128]{1,0,2:T(8,128)(2,1)S(1)} %collective-permute-done), channel_id=1, source_target_pairs={{0,1},{1,2},{2,3},{3,4},{4,5},{5,6},{6,7},{7,8},{8,9},{9,10},{10,1... | collective-permute-start | bytes 98312 | tf_op jit(solution)/shard_map/ppermute | solution.py:64
  50.6 19.2 %collective-permute-start.9 = (bf16[16,8,128]{1,0,2:T(8,128)(2,1)S(1)}, bf16[16,8,128]{1,0,2:T(8,128)(2,1)S(1)}, u32[]{:S(2)}, u32[]{:S(2)}) collective-permute-start(bf16[16,8,128]{1,0,2:T(8,128)(2,1)S(1)} %collective-permute-done.8), channel_id=1, source_target_pairs={{0,15},{1,0},{2,1},{3,2},{4,3},{5,4},{6,5},{7,6},{8,7},{9,8},{10,9... | collective-permute-start | bytes 98312 | tf_op jit(solution)/shard_map/ppermute | solution.py:66
  56.3 14.2 %collective-permute-start.2 = (bf16[16,8,128]{1,0,2:T(8,128)(2,1)S(1)}, bf16[16,8,128]{1,0,2:T(8,128)(2,1)S(1)}, u32[]{:S(2)}, u32[]{:S(2)}) collective-permute-start(bf16[16,8,128]{1,0,2:T(8,128)(2,1)S(1)} %collective-permute-done.1), channel_id=1, source_target_pairs={{0,1},{1,2},{2,3},{3,4},{4,5},{5,6},{6,7},{7,8},{8,9},{9,10},{10,1... | collective-permute-start | bytes 98312 | tf_op jit(solution)/shard_map/ppermute | solution.py:64
  69.8 0.8 copy-start.1
  69.8 14.2 %collective-permute-start.10 = (bf16[16,8,128]{1,0,2:T(8,128)(2,1)S(1)}, bf16[16,8,128]{1,0,2:T(8,128)(2,1)S(1)}, u32[]{:S(2)}, u32[]{:S(2)}) collective-permute-start(bf16[16,8,128]{1,0,2:T(8,128)(2,1)S(1)} %collective-permute-done.9), channel_id=1, source_target_pairs={{0,15},{1,0},{2,1},{3,2},{4,3},{5,4},{6,5},{7,6},{8,7},{9,8},{10,9... | collective-permute-start | bytes 98312 | tf_op jit(solution)/shard_map/ppermute | solution.py:66
  70.6 13.4 %copy-start.2 = (bf16[16,8,128]{1,0,2:T(8,128)(2,1)}, bf16[16,8,128]{1,0,2:T(8,128)(2,1)S(1)}, u32[]{:S(2)}) copy-start(bf16[16,8,128]{1,0,2:T(8,128)(2,1)S(1)} %collective-permute-done.2) | copy-start | bytes 98308
  70.6 14.2 %collective-permute-start.3 = (bf16[16,8,128]{1,0,2:T(8,128)(2,1)S(1)}, bf16[16,8,128]{1,0,2:T(8,128)(2,1)S(1)}, u32[]{:S(2)}, u32[]{:S(2)}) collective-permute-start(bf16[16,8,128]{1,0,2:T(8,128)(2,1)S(1)} %collective-permute-done.2), channel_id=1, source_target_pairs={{0,1},{1,2},{2,3},{3,4},{4,5},{5,6},{6,7},{7,8},{8,9},{9,10},{10,1... | collective-permute-start | bytes 98312 | tf_op jit(solution)/shard_map/ppermute | solution.py:64
  84.0 0.8 copy-start.3
  84.0 14.2 %collective-permute-start.11 = (bf16[16,8,128]{1,0,2:T(8,128)(2,1)S(1)}, bf16[16,8,128]{1,0,2:T(8,128)(2,1)S(1)}, u32[]{:S(2)}, u32[]{:S(2)}) collective-permute-start(bf16[16,8,128]{1,0,2:T(8,128)(2,1)S(1)} %collective-permute-done.10), channel_id=1, source_target_pairs={{0,15},{1,0},{2,1},{3,2},{4,3},{5,4},{6,5},{7,6},{8,7},{9,8},{10,9... | collective-permute-start | bytes 98312 | tf_op jit(solution)/shard_map/ppermute | solution.py:66
  84.8 13.4 %copy-start.4 = (bf16[16,8,128]{1,0,2:T(8,128)(2,1)}, bf16[16,8,128]{1,0,2:T(8,128)(2,1)S(1)}, u32[]{:S(2)}) copy-start(bf16[16,8,128]{1,0,2:T(8,128)(2,1)S(1)} %collective-permute-done.3) | copy-start | bytes 98308
  84.8 14.2 %collective-permute-start.4 = (bf16[16,8,128]{1,0,2:T(8,128)(2,1)S(1)}, bf16[16,8,128]{1,0,2:T(8,128)(2,1)S(1)}, u32[]{:S(2)}, u32[]{:S(2)}) collective-permute-start(bf16[16,8,128]{1,0,2:T(8,128)(2,1)S(1)} %collective-permute-done.3), channel_id=1, source_target_pairs={{0,1},{1,2},{2,3},{3,4},{4,5},{5,6},{6,7},{7,8},{8,9},{9,10},{10,1... | collective-permute-start | bytes 98312 | tf_op jit(solution)/shard_map/ppermute | solution.py:64
  98.2 0.8 copy-start.5
  98.2 14.2 %collective-permute-start.12 = (bf16[16,8,128]{1,0,2:T(8,128)(2,1)S(1)}, bf16[16,8,128]{1,0,2:T(8,128)(2,1)S(1)}, u32[]{:S(2)}, u32[]{:S(2)}) collective-permute-start(bf16[16,8,128]{1,0,2:T(8,128)(2,1)S(1)} %collective-permute-done.11), channel_id=1, source_target_pairs={{0,15},{1,0},{2,1},{3,2},{4,3},{5,4},{6,5},{7,6},{8,7},{9,8},{10,9... | collective-permute-start | bytes 98312 | tf_op jit(solution)/shard_map/ppermute | solution.py:66
  99.0 13.4 %copy-start.6 = (bf16[16,8,128]{1,0,2:T(8,128)(2,1)}, bf16[16,8,128]{1,0,2:T(8,128)(2,1)S(1)}, u32[]{:S(2)}) copy-start(bf16[16,8,128]{1,0,2:T(8,128)(2,1)S(1)} %collective-permute-done.4) | copy-start | bytes 98308
  99.0 14.2 %collective-permute-start.5 = (bf16[16,8,128]{1,0,2:T(8,128)(2,1)S(1)}, bf16[16,8,128]{1,0,2:T(8,128)(2,1)S(1)}, u32[]{:S(2)}, u32[]{:S(2)}) collective-permute-start(bf16[16,8,128]{1,0,2:T(8,128)(2,1)S(1)} %collective-permute-done.4), channel_id=1, source_target_pairs={{0,1},{1,2},{2,3},{3,4},{4,5},{5,6},{6,7},{7,8},{8,9},{9,10},{10,1... | collective-permute-start | bytes 98312 | tf_op jit(solution)/shard_map/ppermute | solution.py:64
  112.5 0.8 copy-start.7
  112.5 14.2 %collective-permute-start.13 = (bf16[16,8,128]{1,0,2:T(8,128)(2,1)S(1)}, bf16[16,8,128]{1,0,2:T(8,128)(2,1)S(1)}, u32[]{:S(2)}, u32[]{:S(2)}) collective-permute-start(bf16[16,8,128]{1,0,2:T(8,128)(2,1)S(1)} %collective-permute-done.12), channel_id=1, source_target_pairs={{0,15},{1,0},{2,1},{3,2},{4,3},{5,4},{6,5},{7,6},{8,7},{9,8},{10,9... | collective-permute-start | bytes 98312 | tf_op jit(solution)/shard_map/ppermute | solution.py:66
  113.3 13.4 %copy-start.8 = (bf16[16,8,128]{1,0,2:T(8,128)(2,1)}, bf16[16,8,128]{1,0,2:T(8,128)(2,1)S(1)}, u32[]{:S(2)}) copy-start(bf16[16,8,128]{1,0,2:T(8,128)(2,1)S(1)} %collective-permute-done.5) | copy-start | bytes 98308
  113.3 14.1 %collective-permute-start.6 = (bf16[16,8,128]{1,0,2:T(8,128)(2,1)S(1)}, bf16[16,8,128]{1,0,2:T(8,128)(2,1)S(1)}, u32[]{:S(2)}, u32[]{:S(2)}) collective-permute-start(bf16[16,8,128]{1,0,2:T(8,128)(2,1)S(1)} %collective-permute-done.5), channel_id=1, source_target_pairs={{0,1},{1,2},{2,3},{3,4},{4,5},{5,6},{6,7},{7,8},{8,9},{9,10},{10,1... | collective-permute-start | bytes 98312 | tf_op jit(solution)/shard_map/ppermute | solution.py:64
  126.7 8.7 %copy-start.9 = (bf16[16,8,128]{1,0,2:T(8,128)(2,1)}, bf16[16,8,128]{1,0,2:T(8,128)(2,1)S(1)}, u32[]{:S(2)}) copy-start(bf16[16,8,128]{1,0,2:T(8,128)(2,1)S(1)} %collective-permute-done.13) | copy-start | bytes 98308
  126.7 8.7 %collective-permute-start.14 = (bf16[16,8,128]{1,0,2:T(8,128)(2,1)S(1)}, bf16[16,8,128]{1,0,2:T(8,128)(2,1)}, u32[]{:S(2)}, u32[]{:S(2)}) collective-permute-start(bf16[16,8,128]{1,0,2:T(8,128)(2,1)S(1)} %collective-permute-done.13), channel_id=1, source_target_pairs={{0,15},{1,0},{2,1},{3,2},{4,3},{5,4},{6,5},{7,6},{8,7},{9,8},{10,9... | collective-permute-start | bytes 98312 | tf_op jit(solution)/shard_map/ppermute | solution.py:66
  127.4 8.0 %copy-start.10 = (bf16[16,8,128]{1,0,2:T(8,128)(2,1)}, bf16[16,8,128]{1,0,2:T(8,128)(2,1)S(1)}, u32[]{:S(2)}) copy-start(bf16[16,8,128]{1,0,2:T(8,128)(2,1)S(1)} %collective-permute-done.6) | copy-start | bytes 98308
  127.4 8.6 %collective-permute-start.7 = (bf16[16,8,128]{1,0,2:T(8,128)(2,1)S(1)}, bf16[16,8,128]{1,0,2:T(8,128)(2,1)}, u32[]{:S(2)}, u32[]{:S(2)}) collective-permute-start(bf16[16,8,128]{1,0,2:T(8,128)(2,1)S(1)} %collective-permute-done.6), channel_id=1, source_target_pairs={{0,1},{1,2},{2,3},{3,4},{4,5},{5,6},{6,7},{7,8},{8,9},{9,10},{10,1... | collective-permute-start | bytes 98312 | tf_op jit(solution)/shard_map/ppermute | solution.py:64
  131.2 21.5 %copy-start.11 = (bf16[128,128]{1,0:T(8,128)(2,1)S(1)}, bf16[128,128]{1,0:T(8,128)(2,1)}, u32[]{:S(2)}) copy-start(bf16[128,128]{1,0:T(8,128)(2,1)} %param.18) | copy-start | bytes 98308
  131.3 21.5 %copy-start.12 = (f32[128]{0:T(128)S(1)}, f32[128]{0:T(128)}, u32[]{:S(2)}) copy-start(f32[128]{0:T(128)} %param.19) | copy-start | bytes 1540
